TPU v7x, 512 devices: a whole 4x8x8 slice. The times are simulated.
512 devices in a mesh: dp: 32 (over x, y_hi, core), fsdp: 16 (over y_lo, z).
Axes of the slice: x: 4, y: 8 (y_hi: 4, y_lo: 2; y = y_hi * 2 + y_lo), z: 8, core: 2. Of those that a mesh axis runs over, the one named last changes fastest.
Arguments:
- hidden: bfloat16 [4, 2048, 16, 4096], P(None, 'dp', 'fsdp'), may hold values from -6 to 6
- frozen_query_rows: bfloat16 [4, 2048, 16, 2048], P(None, 'dp', 'fsdp'), may hold values from -10 to 10
- output_gradient: bfloat16 [4, 2048, 16, 2048], P(None, 'dp', 'fsdp'), may hold values from -6 to 6
- token_log_ratio: float32 [4, 2048, 16], P(None, 'dp', 'fsdp'), may hold values from -0.15625 to 0.15625
- lengths: int32 [4], replicated, may hold values from 1 to 32768, as said below
- response_win_probability: float32 [4], replicated, may hold values from 0.05 to 0.95
- cached_prompt_keys: bfloat16 [1024, 512], P('fsdp'), may hold values from -7.5 to 7.5
- cached_prompt_values: bfloat16 [1024, 512], P('fsdp'), may hold values from -6 to 6
- adapter_down_factor: bfloat16 [4096, 64], P('fsdp'), may hold values from -0.09375 to 0.09375
- adapter_up_factor: bfloat16 [64, 2048], P(None, 'fsdp'), may hold values from -0.125 to 0.125
- attention_norm_gain: bfloat16 [4096], P('fsdp'), may hold values from 0.5 to 1.5
Outputs:
- grad_down: float32 [4096, 64], P('fsdp')
- grad_up: float32 [64, 2048], P(None, 'fsdp')
- seq_ratio: float32 [4], replicated
Inputs may be any that keep to these rules, and one draw needn't show every extreme that they name: The lengths sum to 65472 and the longest is exactly 32768.
All inputs are finite; a program needn't handle non-finite values.
Results may differ from a plain program's by a relative error of at most 0.012.
Values may be sent and summed in bfloat16 or wider, within the bound.
A program may use at most 128 MiB of HBM per device.

v0:
```python
import math
import jax
import jax.numpy as jnp
from jax import lax
from jax.sharding import PartitionSpec as P

HEAD_SIZE = 128
QUERY_HEADS = 16
KEY_VALUE_HEADS = 4
target_scale = 1.0
norm_epsilon = 1e-05


def attend(query_vectors, cotangent, key_rows, value_rows):
    row_count = query_vectors.shape[0]
    queries_per_group = QUERY_HEADS // KEY_VALUE_HEADS
    score_scale = 1.0 / math.sqrt(HEAD_SIZE)
    pieces = []
    for shared_key_head in range(KEY_VALUE_HEADS):
        head_start = shared_key_head * queries_per_group * HEAD_SIZE
        head_stop = head_start + queries_per_group * HEAD_SIZE
        head_query = query_vectors[:, head_start:head_stop].reshape(
            row_count, queries_per_group, HEAD_SIZE
        )
        head_grad = cotangent[:, head_start:head_stop].reshape(
            row_count, queries_per_group, HEAD_SIZE
        )
        head_key = key_rows[:, shared_key_head * HEAD_SIZE : (shared_key_head + 1) * HEAD_SIZE]
        head_value = value_rows[:, shared_key_head * HEAD_SIZE : (shared_key_head + 1) * HEAD_SIZE]
        scores = (
            jnp.einsum("nhd,jd->nhj", head_query, head_key, preferred_element_type=jnp.float32)
            * score_scale
        )
        row_top = jnp.max(scores, axis=2, keepdims=True)
        exponent = jnp.exp(scores - row_top)
        row_total = jnp.sum(exponent, axis=2, keepdims=True)
        weights = exponent.astype(jnp.bfloat16)
        mixed_out = (
            jnp.einsum("nhj,jd->nhd", weights, head_value, preferred_element_type=jnp.float32)
            / row_total
        )
        inner_prod = jnp.sum(head_grad.astype(jnp.float32) * mixed_out, axis=2, keepdims=True)
        grad_prob = jnp.einsum(
            "nhd,jd->nhj", head_grad, head_value, preferred_element_type=jnp.float32
        )
        grad_score = (weights.astype(jnp.float32) / row_total * (grad_prob - inner_prod)).astype(
            jnp.bfloat16
        )
        query_gradient = (
            jnp.einsum("nhj,jd->nhd", grad_score, head_key, preferred_element_type=jnp.float32)
            * score_scale
        )
        pieces.append(query_gradient.reshape(row_count, queries_per_group * HEAD_SIZE))
    return jnp.concatenate(pieces, axis=1).astype(jnp.bfloat16)


def body(
    hidden,
    frozen_query_rows,
    output_gradient,
    token_log_ratio,
    lengths,
    response_win_probability,
    cached_prompt_keys,
    cached_prompt_values,
    adapter_down_factor,
    adapter_up_factor,
    attention_norm_gain,
):
    fsdp_count = lax.axis_size("fsdp")
    dp_index = lax.axis_index("dp")
    fsdp_index = lax.axis_index("fsdp")
    responses, per_device, single, feature_count = hidden.shape
    home_rows = responses * per_device
    local_rows = jnp.arange(per_device, dtype=jnp.int32)
    position = (dp_index * per_device + local_rows) * fsdp_count + fsdp_index
    is_valid = position[None, :] < lengths[:, None]
    partial_value = jnp.sum(jnp.where(is_valid, token_log_ratio[:, :, 0], 0.0), axis=1)
    seq_ratio = lax.psum(partial_value, ("dp", "fsdp"))
    weighting = 2.0 * (seq_ratio - target_scale * (response_win_probability - 0.5)) / responses
    down_full, up_full, gain_full = (
        lax.all_gather(adapter_down_factor, "fsdp", axis=0, tiled=True),
        lax.all_gather(adapter_up_factor, "fsdp", axis=1, tiled=True),
        lax.all_gather(attention_norm_gain, "fsdp", axis=0, tiled=True),
    )
    key_rows, value_rows = (
        lax.all_gather(cached_prompt_keys, "fsdp", axis=0, tiled=True),
        lax.all_gather(cached_prompt_values, "fsdp", axis=0, tiled=True),
    )
    widened = hidden.reshape(home_rows, feature_count).astype(jnp.float32)
    inverse = lax.rsqrt(jnp.mean(widened * widened, axis=1, keepdims=True) + norm_epsilon)
    normed_input = (widened * inverse * gain_full.astype(jnp.float32)).astype(jnp.bfloat16)
    lowrank_hidden = jnp.dot(normed_input, down_full, preferred_element_type=jnp.float32).astype(
        jnp.bfloat16
    )
    row_mask = is_valid.reshape(home_rows)
    row_coef = jnp.repeat(weighting, per_device)
    base_rows = frozen_query_rows.reshape(home_rows, -1)
    cotangent = jnp.where(
        row_mask[:, None],
        row_coef[:, None] * output_gradient.reshape(home_rows, -1).astype(jnp.float32),
        0.0,
    ).astype(jnp.bfloat16)
    query_vectors = (
        base_rows.astype(jnp.float32)
        + jnp.dot(lowrank_hidden, up_full, preferred_element_type=jnp.float32)
    ).astype(jnp.bfloat16)
    query_gradient = attend(query_vectors, cotangent, key_rows, value_rows)
    up_term = jnp.dot(lowrank_hidden.T, query_gradient, preferred_element_type=jnp.float32)
    gradient_lowrank = jnp.dot(
        query_gradient, up_full.T, preferred_element_type=jnp.float32
    ).astype(jnp.bfloat16)
    down_term = jnp.dot(normed_input.T, gradient_lowrank, preferred_element_type=jnp.float32)
    down_sum, up_sum = lax.psum((down_term, up_term), ("dp", "fsdp"))
    down_factor_part = adapter_down_factor.shape[0]
    up_factor_part = adapter_up_factor.shape[1]
    grad_down = lax.dynamic_slice_in_dim(
        down_sum, fsdp_index * down_factor_part, down_factor_part, 0
    )
    grad_up = lax.dynamic_slice_in_dim(up_sum, fsdp_index * up_factor_part, up_factor_part, 1)
    return (grad_down, grad_up, seq_ratio)


def solution(mesh):
    in_specs = (
        P(None, "dp", "fsdp", None),
        P(None, "dp", "fsdp", None),
        P(None, "dp", "fsdp", None),
        P(None, "dp", "fsdp"),
        P(),
        P(),
        P("fsdp", None),
        P("fsdp", None),
        P("fsdp", None),
        P(None, "fsdp"),
        P("fsdp"),
    )
    out_specs = (P("fsdp", None), P(None, "fsdp"), P())
    return jax.shard_map(body, mesh=mesh, in_specs=in_specs, out_specs=out_specs, check_vma=False)
```

profile of v0, /device:TPU:17, one launch (start us, length us, event | category | flops | bytes accessed | tf_op | source)
XLA Modules:
  0.0 574.0 jit_solution(2248930495816452318)
XLA Ops:
  7.2 0.7 all-gather.4.cloned.1.call-update
  8.0 0.7 all-gather.6.cloned.1.call-update
  8.7 0.9 select_reduce_fusion
  9.6 105.0 %psum.21 = f32[4]{0:T(128)S(1)} all-reduce(f32[4]{0:T(128)S(1)} %get-tuple-element.5), channel_id=1, replica_groups=mesh['dp'=32,'fsdp'=16] {'dp','fsdp'}, use_global_device_ids=true, to_apply=%region_4.5 | all-reduce | flops 4 | bytes 32 | tf_op jit(solution)/shard_map/psum | solution.py:79
  116.1 2.1 multiply_reduce_fusion
  118.3 24.8 %all-gather = bf16[16,1,256]{2,1,0:T(2,128)(2,1)S(1)} all-gather(bf16[1,1,256]{2,1,0:T(2,128)(2,1)S(1)} %reshape.122), channel_id=1, replica_groups=mesh['dp'=32,'fsdp'=16] {'fsdp'}, dimensions={0}, use_global_device_ids=true | all-gather | bytes 8704 | tf_op jit(solution)/shard_map/all_gather | solution.py:84
  143.1 2.2 fusion.1
  145.7 1.3 slice_bitcast_fusion.35
  147.0 1.7 reshape.117
  148.7 1.7 reshape.114
  150.5 1.7 reshape.111
  152.2 0.8 reshape.108
  152.9 24.4 %all_gather.17 = bf16[64,2048]{1,0:T(8,128)(2,1)S(1)} all-gather(bf16[64,128]{1,0:T(8,128)(2,1)S(1)} %copy-done.17), channel_id=1, replica_groups=mesh['dp'=32,'fsdp'=16] {'fsdp'}, dimensions={1}, use_global_device_ids=true | all-gather | bytes 278528 | tf_op jit(solution)/shard_map/all_gather | solution.py:83
  177.3 27.5 %all_gather.16 = bf16[4096,64]{0,1:T(8,128)(2,1)S(1)} all-gather(bf16[256,64]{0,1:T(8,128)(2,1)S(1)} %copy-done.16), channel_id=1, replica_groups=mesh['dp'=32,'fsdp'=16] {'fsdp'}, dimensions={0}, use_global_device_ids=true | all-gather | bytes 557056 | tf_op jit(solution)/shard_map/all_gather | solution.py:82
  204.8 0.8 convolution_convert_fusion.1
  206.2 0.9 slice_bitcast_fusion.11
  207.1 1.7 multiply_reduce_fusion.4
  208.8 2.0 copy-done
  210.8 0.9 fusion.2
  211.9 3.0 fusion.39
  215.0 0.8 fusion.26
  216.4 1.9 multiply_reduce_fusion.1
  218.3 1.9 copy-done.1
  220.3 0.9 fusion.8
  221.2 0.8 copy.39
  222.0 3.1 fusion.30
  225.1 0.8 fusion.29
  226.6 1.8 multiply_reduce_fusion.2
  228.4 2.0 copy-done.2
  230.3 0.9 fusion.6
  231.3 0.8 copy.35
  232.1 3.1 fusion.33
  235.2 0.8 fusion.28
  236.6 1.8 multiply_reduce_fusion.3
  238.4 1.9 copy-done.3
  240.4 1.1 fusion.4
  241.5 0.8 copy.31
  242.3 3.1 fusion.36
  245.4 0.8 fusion.27
  246.9 4.8 fusion.21
  251.7 4.8 fusion.24
  256.5 4.8 fusion.23
  261.3 4.8 fusion.22
  266.2 3.6 fusion.25
  269.8 2.2 fusion.70
  272.0 292.6 %all-reduce.3.cloned.1.call-done = (f32[4096,64]{0,1:T(8,128)}, f32[64,2048]{1,0:T(8,128)}) async-done(((f32[4096,64]{0,1:T(8,128)}, f32[64,2048]{1,0:T(8,128)}), (f32[4096,64]{0,1:T(8,128)}, f32[64,2048]{1,0:T(8,128)})) %all-reduce.3.cloned.1.call-update) | async-done | bytes 1572880 | tf_op jit(solution)/shard_map/psum | solution.py:114
  564.6 1.5 constant_dynamic-slice_fusion.1
  566.1 1.4 constant_dynamic-slice_fusion
  (82 shorter events, 5.7 us)
Async XLA Ops:
  7.2 138.2 %copy-start.6 = (bf16[4,64,1,2048]{3,1,2,0:T(8,128)(2,1)S(1)}, bf16[4,64,1,2048]{3,1,2,0:T(8,128)(2,1)}, u32[]{:S(2)}) copy-start(bf16[4,64,1,2048]{3,1,2,0:T(8,128)(2,1)} %param.13) | copy-start | bytes 3145732
  7.2 199.9 %all-gather.4.cloned.1.call-start = ((), (), s32[]{:S(2)}) async-start(), calls=%async_computation | async-start | bytes 1114112 | tf_op jit(solution)/shard_map/all_gather | solution.py:87
  7.9 204.0 %all-gather.6.cloned.1.call-start = ((), (), s32[]{:S(2)}) async-start(), calls=%async_computation.1 | async-start | bytes 1114112 | tf_op jit(solution)/shard_map/all_gather | solution.py:88
  8.7 555.9 %all-reduce.3.cloned.1.call-start = ((), (), s32[]{:S(2)}) async-start(), calls=%async_computation.2 | async-start | bytes 3145728 | tf_op jit(solution)/shard_map/psum | solution.py:114
  114.6 3.7 copy-start.31
  145.3 7.6 %copy-start.17 = (bf16[64,128]{1,0:T(8,128)(2,1)S(1)}, bf16[64,128]{1,0:T(8,128)(2,1)}, u32[]{:S(2)}) copy-start(bf16[64,128]{1,0:T(8,128)(2,1)} %param.20) | copy-start | bytes 49156
  145.4 32.0 %copy-start.16 = (bf16[256,64]{0,1:T(8,128)(2,1)S(1)}, bf16[256,64]{0,1:T(8,128)(2,1)}, u32[]{:S(2)}) copy-start(bf16[256,64]{0,1:T(8,128)(2,1)} %param.19) | copy-start | bytes 98308
  145.7 59.9 %copy-start.5 = (bf16[4,64,1,2048]{3,1,2,0:T(8,128)(2,1)S(1)}, bf16[4,64,1,2048]{3,1,2,0:T(8,128)(2,1)}, u32[]{:S(2)}) copy-start(bf16[4,64,1,2048]{3,1,2,0:T(8,128)(2,1)} %param.12) | copy-start | bytes 3145732
  205.6 0.6 copy-start.14
  208.8 2.0 copy-start
  210.8 4.2 copy-start.10
  211.7 6.6 %copy-start.18 = (f32[256,4]{0,1:T(4,128)}, f32[256,4]{0,1:T(4,128)S(1)}, u32[]{:S(2)}) copy-start(f32[256,4]{0,1:T(4,128)S(1)} %fusion.2) | copy-start | bytes 12292
  216.4 5.6 copy-start.4
  218.3 1.9 copy-start.1
  221.2 0.8 copy-start.19
  222.0 3.1 copy-start.9
  222.0 3.1 copy-start.11
  228.4 2.0 copy-start.2
  231.3 0.8 copy-start.21
  232.1 3.1 copy-start.8
  232.1 3.1 copy-start.12
  238.4 1.9 copy-start.3
  241.5 0.8 copy-start.23
  242.3 3.1 copy-start.7
  242.3 3.1 copy-start.13
  246.9 4.8 copy-start.20
  246.9 4.8 copy-start.25
  251.7 4.8 copy-start.22
  251.7 4.8 copy-start.26
  256.5 4.8 copy-start.24
  256.5 4.8 copy-start.27
  266.2 3.7 copy-start.15
  266.2 3.7 copy-start.28
  266.2 3.7 copy-start.29
  266.2 3.7 copy-start.30
Sparse Core Ops, SparseCore 0:
  10.1 66.9 all-gather.3
  79.2 69.6 all-gather.5
  272.2 292.3 all-reduce.2
where the time goes:
time: 575 us; the launch traced here: 574 us
  waiting for transfers between devices  294 us (51%)
  blocking collectives  182 us (32%)
  matrix products  45.8 us (8%)
  local copies, waits for them, and re-layouts  25.3 us (4%)
  between operations  14.1 us (2%)
  other arithmetic  13.1 us (2%)
    psum x1, waiting for transfers between devices, body(): down_sum, up_sum = lax.psum((down_term, up_term), ('dp', 'fsdp'))  293 us
    psum x1, blocking collectives, body(): seq_ratio = lax.psum(partial_value, ('dp', 'fsdp'))  105 us
    all_gather x1, blocking collectives, body(): lax.all_gather(adapter_down_factor, 'fsdp', axis=0, tiled=True)  27.5 us
    all_gather x1, blocking collectives, body(): lax.all_gather(attention_norm_gain, 'fsdp', axis=0, tiled=True)  24.8 us
    all_gather x1, blocking collectives, body(): lax.all_gather(adapter_up_factor, 'fsdp', axis=1, tiled=True)  24.4 us
    dot_general x4, matrix products, attend(): jnp.einsum('nhj,jd->nhd', grad_score, head_key, preferred_element_type=jn...  19.2 us
    dot_general x4, matrix products, attend(): jnp.einsum('nhj,jd->nhd', weights, head_value, preferred_element_type=jnp...  12.3 us
  transfers between devices with their start and end apart: 3, of which 1 were waited for; matrix products, arithmetic and copies ran while one was open for 3% of the time, Pallas kernels for 0%

commit v1 on v0

--- a/solution.py
+++ b/solution.py
@@ -79,7 +79,10 @@
     seq_ratio = lax.psum(partial_value, ("dp", "fsdp"))
     weighting = 2.0 * (seq_ratio - target_scale * (response_win_probability - 0.5)) / responses
     down_full, up_full, gain_full = (
-        lax.all_gather(adapter_down_factor, "fsdp", axis=0, tiled=True),
+        jnp.concatenate(
+            lax.all_to_all(jnp.stack([adapter_down_factor] * lax.axis_size("fsdp")), "fsdp", 0, 0),
+            axis=0,
+        ),
         lax.all_gather(adapter_up_factor, "fsdp", axis=1, tiled=True),
         lax.all_gather(attention_norm_gain, "fsdp", axis=0, tiled=True),
     )

time: 575 us -> 539 us (0.937)
  waiting for transfers between devices: 294 us -> 274 us
  blocking collectives: 182 us -> 169 us
  starting transfers between devices: 0.11 us -> 11.3 us
  local copies, waits for them, and re-layouts: 25.3 us -> 14.6 us
    all_gather x1 -> x0, blocking collectives: 27.5 us -> none  [body(): lax.all_gather(adapter_down_factor, 'fsdp', axis=0, tiled=True)]
    psum x1, waiting for transfers between devices: 293 us -> 273 us  [body(): down_sum, up_sum = lax.psum((down_term, up_term), ('dp', 'fsdp'))]
    all_to_all x0 -> x1, starting transfers between devices: none -> 11.2 us  [body(): lax.all_to_all(jnp.stack([adapter_down_factor] * lax.axis_size('fsdp')),...]
    all_gather x1, blocking collectives: 24.8 us -> 34.7 us  [body(): lax.all_gather(attention_norm_gain, 'fsdp', axis=0, tiled=True)]
    unnamed x67 -> x36, local copies, waits for them, and re-layouts: 10.9 us -> 4.41 us
    reshape x4 -> x1, local copies, waits for them, and re-layouts: 5.92 us -> 0.03 us  [body(): jnp.concatenate(lax.all_to_all(jnp.stack([adapter_down_factor] * lax.axis...]
  transfers between devices with their start and end apart: 3 -> 4, of which waited for: 1 -> 1; matrix products, arithmetic and copies ran while one was open for 3% -> 5% of each run, Pallas kernels for 0% -> 0%
where the time goes in v1:
time: 539 us; the launch traced here: 538 us
  waiting for transfers between devices  274 us (51%)
  blocking collectives  169 us (31%)
  matrix products  43.4 us (8%)
  local copies, waits for them, and re-layouts  14.6 us (3%)
  between operations  14 us (3%)
  other arithmetic  11.5 us (2%)
  starting transfers between devices  11.3 us (2%)
    psum x1, waiting for transfers between devices, body(): down_sum, up_sum = lax.psum((down_term, up_term), ('dp', 'fsdp'))  273 us
    psum x1, blocking collectives, body(): seq_ratio = lax.psum(partial_value, ('dp', 'fsdp'))  108 us
    all_gather x1, blocking collectives, body(): lax.all_gather(attention_norm_gain, 'fsdp', axis=0, tiled=True)  34.7 us
    all_gather x1, blocking collectives, body(): lax.all_gather(adapter_up_factor, 'fsdp', axis=1, tiled=True)  26.3 us
    dot_general x4, matrix products, attend(): jnp.einsum('nhj,jd->nhd', grad_score, head_key, preferred_element_type=jn...  18.2 us
    dot_general x4, matrix products, attend(): jnp.einsum('nhj,jd->nhd', weights, head_value, preferred_element_type=jnp...  13 us
    all_to_all x1, starting transfers between devices, body(): lax.all_to_all(jnp.stack([adapter_down_factor] * lax.axis_size('fsdp')),...  11.2 us
  transfers between devices with their start and end apart: 4, of which 1 were waited for; matrix products, arithmetic and copies ran while one was open for 5% of the time, Pallas kernels for 0%

profile of v1, /device:TPU:17, one launch (start us, length us, event | category | flops | bytes accessed | tf_op | source)
XLA Modules:
  0.0 538.0 jit_solution(10086134916646878418)
XLA Ops:
  7.3 0.7 all-gather.4.cloned.1.call-update
  8.0 1.6 stack.2
  9.6 11.2 %all-to-all-start = ((bf16[16,256,64]{1,2,0:T(8,128)(2,1)}), bf16[16,256,64]{1,2,0:T(8,128)(2,1)S(1)}, u32[]{:S(2)}, u32[]{:S(2)}) async-start(bf16[16,256,64]{1,2,0:T(8,128)(2,1)} %stack.2), calls=%async_computation | async-start | bytes 1048576 | tf_op jit(solution)/shard_map/all_to_all | solution.py:83
  20.8 0.7 all-gather.6.cloned.1.call-update
  21.5 0.7 reshape.140
  22.2 34.7 %all-gather = bf16[16,1,256]{2,1,0:T(2,128)(2,1)S(1)} all-gather(bf16[1,1,256]{2,1,0:T(2,128)(2,1)S(1)} %reshape.140), channel_id=1, replica_groups=mesh['dp'=32,'fsdp'=16] {'fsdp'}, dimensions={0}, use_global_device_ids=true | all-gather | bytes 8704 | tf_op jit(solution)/shard_map/all_gather | solution.py:87
  56.9 2.1 multiply_reduce_fusion
  59.1 0.1 rsqrt.13
  59.1 2.0 multiply_convert_fusion.4
  61.1 26.3 %all_gather.13 = bf16[64,2048]{1,0:T(8,128)(2,1)S(1)} all-gather(bf16[64,128]{1,0:T(8,128)(2,1)S(1)} %copy-done.11), channel_id=1, replica_groups=mesh['dp'=32,'fsdp'=16] {'fsdp'}, dimensions={1}, use_global_device_ids=true | all-gather | bytes 278528 | tf_op jit(solution)/shard_map/all_gather | solution.py:86
  87.5 0.2 select_reduce_fusion
  87.7 108.0 %psum.21 = f32[4]{0:T(128)S(1)} all-reduce(f32[4]{0:T(128)S(1)} %get-tuple-element.5), channel_id=1, replica_groups=mesh['dp'=32,'fsdp'=16] {'dp','fsdp'}, use_global_device_ids=true, to_apply=%region_4.5 | all-reduce | flops 4 | bytes 32 | tf_op jit(solution)/shard_map/psum | solution.py:79
  195.8 0.1 lt.29
  195.9 1.5 fusion.12
  197.5 0.9 fusion.66
  198.3 1.8 copy.97
  200.1 1.8 copy.104
  201.9 0.8 copy.111
  202.7 0.1 copy.118
  202.9 2.0 fusion.1
  204.9 2.4 convolution_convert_fusion.1
  207.3 0.5 fusion.10
  207.8 0.1 slice_bitcast_fusion.11
  207.9 1.8 multiply_reduce_fusion.4
  209.8 0.8 multiply_reduce_fusion.3
  210.6 0.9 fusion.2
  211.5 0.2 copy-done.4
  211.7 0.9 fusion.4
  212.7 0.4 copy-done.2
  213.1 0.8 multiply_reduce_fusion.2
  213.9 0.9 fusion.6
  214.8 1.0 copy-done.3
  215.8 0.8 multiply_reduce_fusion.1
  216.6 1.9 copy-done.1
  218.5 0.9 fusion.8
  219.5 3.2 fusion.29
  222.7 4.9 fusion.25
  227.6 3.4 fusion.30
  231.0 4.2 fusion.26
  235.2 3.2 fusion.31
  238.4 4.1 fusion.27
  242.6 3.2 fusion.32
  245.8 5.0 fusion.28
  250.8 2.2 fusion.54
  253.0 2.9 fusion.33
  255.9 272.6 %all-reduce.3.cloned.1.call-done = (f32[4096,64]{0,1:T(8,128)}, f32[64,2048]{1,0:T(8,128)}) async-done(((f32[4096,64]{0,1:T(8,128)}, f32[64,2048]{1,0:T(8,128)}), (f32[4096,64]{0,1:T(8,128)}, f32[64,2048]{1,0:T(8,128)})) %all-reduce.3.cloned.1.call-update) | async-done | bytes 1572880 | tf_op jit(solution)/shard_map/psum | solution.py:117
  528.6 1.5 constant_dynamic-slice_fusion.1
  530.1 1.4 constant_dynamic-slice_fusion
  (44 shorter events, 0.5 us)
Async XLA Ops:
  7.2 52.0 %copy-start = (bf16[4,64,1,4096]{3,1,2,0:T(8,128)(2,1)S(1)}, bf16[4,64,1,4096]{3,1,2,0:T(8,128)(2,1)}, u32[]{:S(2)}) copy-start(bf16[4,64,1,4096]{3,1,2,0:T(8,128)(2,1)} %param.11) | copy-start | bytes 6291460
  7.2 54.0 %copy-start.11 = (bf16[64,128]{1,0:T(8,128)(2,1)S(1)}, bf16[64,128]{1,0:T(8,128)(2,1)}, u32[]{:S(2)}) copy-start(bf16[64,128]{1,0:T(8,128)(2,1)} %param.20) | copy-start | bytes 49156
  7.2 80.3 %copy-start.12 = (f32[4,64,1]{1,2,0:T(1,128)S(1)}, f32[4,64,1]{1,2,0:T(1,128)}, u32[]{:S(2)}) copy-start(f32[4,64,1]{1,2,0:T(1,128)} %param.14) | copy-start | bytes 3076
  7.2 80.3 %copy-start.13 = (s32[4]{0:T(128)S(1)}, s32[4]{0:T(128)}, u32[]{:S(2)}) copy-start(s32[4]{0:T(128)} %param.15) | copy-start | bytes 52
  7.2 188.5 %copy-start.14 = (f32[4]{0:T(128)S(1)}, f32[4]{0:T(128)}, u32[]{:S(2)}) copy-start(f32[4]{0:T(128)} %param.16) | copy-start | bytes 52
  7.2 200.7 %all-gather.4.cloned.1.call-start = ((), (), s32[]{:S(2)}) async-start(), calls=%async_computation.1 | async-start | bytes 1114112 | tf_op jit(solution)/shard_map/all_gather | solution.py:90
  9.6 195.3 %all-to-all-start = ((bf16[16,256,64]{1,2,0:T(8,128)(2,1)}), bf16[16,256,64]{1,2,0:T(8,128)(2,1)S(1)}, u32[]{:S(2)}, u32[]{:S(2)}) async-start(bf16[16,256,64]{1,2,0:T(8,128)(2,1)} %stack.2), calls=%async_computation | async-start | bytes 1048576 | tf_op jit(solution)/shard_map/all_to_all | solution.py:83
  20.7 198.8 %all-gather.6.cloned.1.call-start = ((), (), s32[]{:S(2)}) async-start(), calls=%async_computation.2 | async-start | bytes 1114112 | tf_op jit(solution)/shard_map/all_gather | solution.py:91
  21.5 507.1 %all-reduce.3.cloned.1.call-start = ((), (), s32[]{:S(2)}) async-start(), calls=%async_computation.3 | async-start | bytes 3145728 | tf_op jit(solution)/shard_map/psum | solution.py:117
  195.7 9.2 %copy-start.16 = (f32[4]{0:T(128)}, f32[4]{0:T(128)S(1)}, u32[]{:S(2)}) copy-start(f32[4]{0:T(128)S(1)} %psum.21) | copy-start | bytes 52
  204.9 2.5 copy-start.6
  207.9 1.8 copy-start.7
  209.8 2.0 copy-start.4
  210.6 2.5 copy-start.2
  213.8 2.0 copy-start.3
  215.8 3.7 copy-start.10
  216.6 1.9 copy-start.1
  222.7 4.9 copy-start.9
  231.0 4.2 copy-start.8
  245.8 5.0 copy-start.15
  245.8 7.2 %copy-start.5 = (bf16[256,4096]{1,0:T(8,128)(2,1)S(1)}, bf16[256,4096]{1,0:T(8,128)(2,1)}, u32[]{:S(2)}) copy-start(bf16[256,4096]{1,0:T(8,128)(2,1)} %fusion.1) | copy-start | bytes 6291460
Sparse Core Ops, SparseCore 0:
  10.1 67.7 all-gather.3
  80.0 69.3 all-gather.5
  256.1 272.4 all-reduce.2
